TPU v7x, 32 devices: a whole 2x2x4 slice. The times are simulated.
32 devices in a mesh: fsdp: 2 (over core), ctx: 4 (over y, x), tp: 4 (over z).
Axes of the slice: x: 2, y: 2, z: 4, core: 2. Of those that a mesh axis runs over, the one named last changes fastest.
Arguments:
- tokens: bfloat16 [4096, 2048], P(('fsdp', 'ctx')), may hold values from -6 to 6
- attn_gain: bfloat16 [2048], P(('fsdp', 'ctx')), may hold values from 0.099609375 to 1.8984375
- w_query: bfloat16 [2048, 2048], P(('fsdp', 'ctx'), 'tp'), may hold values from -0.125 to 0.125
- w_key: bfloat16 [2048, 256], P(('fsdp', 'ctx'), 'tp'), may hold values from -0.125 to 0.125
- w_value: bfloat16 [2048, 256], P(('fsdp', 'ctx'), 'tp'), may hold values from -0.125 to 0.125
- w_out: bfloat16 [2048, 2048], P('tp', ('fsdp', 'ctx')), may hold values from -1 to 1
- mlp_gain: bfloat16 [2048], P(('fsdp', 'ctx')), may hold values from 0.099609375 to 1.8984375
- w_gate: bfloat16 [2048, 5632], P(('fsdp', 'ctx'), 'tp'), may hold values from -0.125 to 0.125
- w_up: bfloat16 [2048, 5632], P(('fsdp', 'ctx'), 'tp'), may hold values from -0.125 to 0.125
- w_down: bfloat16 [5632, 2048], P('tp', ('fsdp', 'ctx')), may hold values from -0.15625 to 0.15625
- cotangent: bfloat16 [4096, 2048], P(('fsdp', 'ctx')), may hold values from -6 to 6
- positions: int32 [4096], P(('fsdp', 'ctx')), may hold values from 0 to 1023, as said below
- segments: int32 [4096], P(('fsdp', 'ctx')), may hold values from 0 to 4095, as said below
Outputs:
- output: bfloat16 [4096, 2048], P(('fsdp', 'ctx'))
- input_grad: bfloat16 [4096, 2048], P(('fsdp', 'ctx'))
- attn_gain_grad: float32 [2048], P(('fsdp', 'ctx'))
- w_query_grad: float32 [2048, 2048], P(('fsdp', 'ctx'), 'tp')
- w_key_grad: float32 [2048, 256], P(('fsdp', 'ctx'), 'tp')
- w_value_grad: float32 [2048, 256], P(('fsdp', 'ctx'), 'tp')
- w_out_grad: float32 [2048, 2048], P('tp', ('fsdp', 'ctx'))
- mlp_gain_grad: float32 [2048], P(('fsdp', 'ctx'))
- w_gate_grad: float32 [2048, 5632], P(('fsdp', 'ctx'), 'tp')
- w_up_grad: float32 [2048, 5632], P(('fsdp', 'ctx'), 'tp')
- w_down_grad: float32 [5632, 2048], P('tp', ('fsdp', 'ctx'))
Inputs may be any that keep to these rules, and one draw needn't show every extreme that they name: Every sequence is cut into 8 stretches of 128 consecutive positions, laid in increasing order inside a stretch; its stretches lie on one index of fsdp, two on each index of ctx, in an order drawn from the seed; each device holds 4 stretches, those of one sequence side by side. `segments`: A document is a run of consecutive positions of one sequence with one number, 200 to 2000 long except the last of a sequence, which may be shorter; documents of different sequences have different numbers.
All inputs are finite; a program needn't handle non-finite values.
Results may differ from a plain program's by a relative error of at most 0.025.
Values may be sent and summed in bfloat16 or wider, within the bound.
A program may use at most 192 MiB of HBM per device.

v0:
```python
import jax
import jax.numpy as jnp
from jax import lax
from jax.sharding import PartitionSpec as P

H = 32
KVH = 4
HD = 64
EPSILON = 1e-05
THETA_BASE = 10000.0
MASKED_SCORE = -1e30


def shifted(value, axis, steps):
    count = lax.axis_size(axis)
    pairs = [(source, (source + steps) % count) for source in range(count)]
    return lax.ppermute(value, axis, pairs)


def rope_tables(token_pos, half_size):
    frequency = THETA_BASE ** (-jnp.arange(half_size, dtype=jnp.float32) / half_size)
    angles = token_pos.astype(jnp.float32)[:, None] * frequency[None, :]
    return (jnp.cos(angles), jnp.sin(angles))


def rotate(head_rows, cosine, sine):
    half_size = head_rows.shape[-1] // 2
    first_half = head_rows[..., :half_size]
    second_half = head_rows[..., half_size:]
    cos_rows = cosine[:, None, :]
    sin_rows = sine[:, None, :]
    return jnp.concatenate(
        [
            first_half * cos_rows - second_half * sin_rows,
            second_half * cos_rows + first_half * sin_rows,
        ],
        axis=-1,
    )


def rotate_back(head_rows, cosine, sine):
    half_size = head_rows.shape[-1] // 2
    first_half = head_rows[..., :half_size]
    second_half = head_rows[..., half_size:]
    cos_rows = cosine[:, None, :]
    sin_rows = sine[:, None, :]
    return jnp.concatenate(
        [
            first_half * cos_rows + second_half * sin_rows,
            second_half * cos_rows - first_half * sin_rows,
        ],
        axis=-1,
    )


def project(left_side, right_side):
    return jnp.dot(left_side, right_side, preferred_element_type=jnp.float32)


def project_back(left_side, right_side):
    return lax.dot_general(
        left_side, right_side, (((1,), (1,)), ((), ())), preferred_element_type=jnp.float32
    )


def weight_grad(left_side, right_side):
    return lax.dot_general(
        left_side, right_side, (((0,), (0,)), ((), ())), preferred_element_type=jnp.float32
    )


def rms_norm(rows_in, gain_vec):
    inv_rms = lax.rsqrt(jnp.mean(rows_in * rows_in, axis=-1, keepdims=True) + EPSILON)
    unit_rows = rows_in * inv_rms
    return (unit_rows * gain_vec, unit_rows, inv_rms)


def rms_norm_back(gradient, gain_vec, unit_rows, inv_rms):
    gain_grad = jnp.sum(gradient * unit_rows, axis=0)
    scaled_grad = gradient * gain_vec
    return (
        inv_rms
        * (scaled_grad - unit_rows * jnp.mean(scaled_grad * unit_rows, axis=-1, keepdims=True)),
        gain_grad,
    )


def pair_mask(query_pos, query_seg, key_pos, key_seg):
    return (query_seg[:, None] == key_seg[None, :]) & (key_pos[None, :] <= query_pos[:, None])


def split_block(kv_block, kv_heads):
    key_rows = kv_block[:, : kv_heads * HD].reshape(-1, kv_heads, HD)
    value_rows = kv_block[:, kv_heads * HD :].reshape(-1, kv_heads, HD)
    return (key_rows, value_rows)


def attend_block(state_in, queries, kv_block, visible):
    row_top, row_total, output_sum = state_in
    key_rows, value_rows = split_block(kv_block, queries.shape[1])
    scores = jnp.einsum(
        "qkgd,pkd->kgqp", queries, key_rows, preferred_element_type=jnp.float32
    ) * HD ** (-0.5)
    scores = jnp.where(visible, scores, MASKED_SCORE)
    new_top = jnp.maximum(row_top, jnp.max(scores, axis=-1))
    weights = jnp.where(visible, jnp.exp(scores - new_top[..., None]), 0.0)
    decay_factor = jnp.exp(row_top - new_top)
    row_total = row_total * decay_factor + jnp.sum(weights, axis=-1)
    mixed_heads = jnp.einsum(
        "kgqp,pkd->qkgd",
        weights.astype(jnp.bfloat16),
        value_rows,
        preferred_element_type=jnp.float32,
    )
    output_sum = output_sum * jnp.transpose(decay_factor, (2, 0, 1))[..., None] + mixed_heads
    return (new_top, row_total, output_sum)


def block_grads(queries, out_grad, kv_block, visible, log_total, delta_rows):
    key_rows, value_rows = split_block(kv_block, queries.shape[1])
    scale_factor = HD ** (-0.5)
    scores = (
        jnp.einsum("qkgd,pkd->kgqp", queries, key_rows, preferred_element_type=jnp.float32)
        * scale_factor
    )
    probs_full = jnp.where(
        visible, jnp.exp(jnp.where(visible, scores, MASKED_SCORE) - log_total[..., None]), 0.0
    )
    value_grad = jnp.einsum(
        "kgqp,qkgd->pkd",
        probs_full.astype(jnp.bfloat16),
        out_grad,
        preferred_element_type=jnp.float32,
    )
    prob_grad = jnp.einsum(
        "qkgd,pkd->kgqp", out_grad, value_rows, preferred_element_type=jnp.float32
    )
    score_grad = (probs_full * (prob_grad - delta_rows[..., None])).astype(jnp.bfloat16)
    query_grad = (
        jnp.einsum("kgqp,pkd->qkgd", score_grad, key_rows, preferred_element_type=jnp.float32)
        * scale_factor
    )
    key_grad = (
        jnp.einsum("kgqp,qkgd->pkd", score_grad, queries, preferred_element_type=jnp.float32)
        * scale_factor
    )
    block_rows = kv_block.shape[0]
    return (
        query_grad,
        jnp.concatenate(
            [key_grad.reshape(block_rows, -1), value_grad.reshape(block_rows, -1)], axis=-1
        ),
    )


def shards(
    tokens,
    attn_gain,
    w_query,
    w_key,
    w_value,
    w_out,
    mlp_gain,
    w_gate,
    w_up,
    w_down,
    cotangent,
    positions,
    segments,
):
    token_rows = tokens.shape[0]
    gain_one, query_w, key_w, value_w, out_w = (
        lax.all_gather(attn_gain, ("fsdp", "ctx"), axis=0, tiled=True),
        lax.all_gather(w_query, ("fsdp", "ctx"), axis=0, tiled=True),
        lax.all_gather(w_key, ("fsdp", "ctx"), axis=0, tiled=True),
        lax.all_gather(w_value, ("fsdp", "ctx"), axis=0, tiled=True),
        lax.all_gather(w_out, ("fsdp", "ctx"), axis=1, tiled=True),
    )
    gain_two, gate_w, up_w, down_w = (
        lax.all_gather(mlp_gain, ("fsdp", "ctx"), axis=0, tiled=True),
        lax.all_gather(w_gate, ("fsdp", "ctx"), axis=0, tiled=True),
        lax.all_gather(w_up, ("fsdp", "ctx"), axis=0, tiled=True),
        lax.all_gather(w_down, ("fsdp", "ctx"), axis=1, tiled=True),
    )
    head_count = query_w.shape[1] // HD
    kv_heads = key_w.shape[1] // HD
    groups = H // KVH
    cosine, sine = rope_tables(positions, HD // 2)
    token_float = tokens.astype(jnp.float32)
    gain_one_float = gain_one.astype(jnp.float32)
    normed_one, unit_one, inv_one = rms_norm(token_float, gain_one_float)
    normed_low = normed_one.astype(jnp.bfloat16)
    query_lin = project(normed_low, query_w)
    key_lin = project(normed_low, key_w)
    value_low = project(normed_low, value_w).astype(jnp.bfloat16)
    query_rot = rotate(query_lin.reshape(token_rows, head_count, HD), cosine, sine).astype(
        jnp.bfloat16
    )
    key_rot = rotate(key_lin.reshape(token_rows, kv_heads, HD), cosine, sine).astype(jnp.bfloat16)
    queries = query_rot.reshape(token_rows, kv_heads, groups, HD)
    kv_local = jnp.concatenate([key_rot.reshape(token_rows, kv_heads * HD), value_low], axis=-1)
    key_positions, key_segments = (
        lax.all_gather(positions, "ctx", axis=0, tiled=True),
        lax.all_gather(segments, "ctx", axis=0, tiled=True),
    )
    my_index = lax.axis_index("ctx")
    cycle_size = lax.axis_size("ctx")

    def block_marks(source):
        start_row = source * token_rows
        return pair_mask(
            positions,
            segments,
            lax.dynamic_slice_in_dim(key_positions, start_row, token_rows),
            lax.dynamic_slice_in_dim(key_segments, start_row, token_rows),
        )

    start_state = (
        jnp.full((kv_heads, groups, token_rows), MASKED_SCORE, jnp.float32),
        jnp.zeros((kv_heads, groups, token_rows), jnp.float32),
        jnp.zeros((token_rows, kv_heads, groups, HD), jnp.float32),
    )

    def forward_block(state_in, kv_block, source):
        visible = block_marks(source)
        return attend_block(state_in, queries, kv_block, visible)

    def cycle_step(state_in, step_index):
        attn_state, kv_block = state_in
        attn_state = forward_block(attn_state, kv_block, (my_index - step_index) % cycle_size)
        passed = shifted(kv_block, "ctx", 1)
        return ((attn_state, passed), kv_block)

    (attn_state, last_block), kept_blocks = lax.scan(
        cycle_step, (start_state, kv_local), jnp.arange(cycle_size - 1)
    )
    attn_state = forward_block(attn_state, last_block, (my_index + 1) % cycle_size)
    kv_blocks = jnp.concatenate([kept_blocks, last_block[None]], axis=0)
    sources = (my_index - jnp.arange(cycle_size)) % cycle_size
    row_top, row_total, output_sum = attn_state
    attended = output_sum / jnp.transpose(row_total, (2, 0, 1))[..., None]
    log_total = row_top + jnp.log(row_total)
    attended_low = attended.reshape(token_rows, head_count * HD).astype(jnp.bfloat16)
    middle = token_float + lax.psum(project(attended_low, out_w).astype(jnp.bfloat16), "tp").astype(
        jnp.float32
    )
    gain_two_float = gain_two.astype(jnp.float32)
    normed_two, unit_two, inv_two = rms_norm(middle, gain_two_float)
    normed_two_low = normed_two.astype(jnp.bfloat16)
    gate_lin = project(normed_two_low, gate_w)
    up_lin = project(normed_two_low, up_w)
    hidden_low = (jax.nn.silu(gate_lin) * up_lin).astype(jnp.bfloat16)
    result = middle + lax.psum(project(hidden_low, down_w).astype(jnp.bfloat16), "tp").astype(
        jnp.float32
    )
    output = result.astype(jnp.bfloat16)
    hidden_grad = project_back(cotangent, down_w)
    down_w_grad = weight_grad(hidden_low, cotangent)
    sigmoid_gate = jax.nn.sigmoid(gate_lin)
    gate_grad_low = (
        hidden_grad * up_lin * sigmoid_gate * (1.0 + gate_lin * (1.0 - sigmoid_gate))
    ).astype(jnp.bfloat16)
    up_grad_low = (hidden_grad * gate_lin * sigmoid_gate).astype(jnp.bfloat16)
    normed_two_grad = lax.psum(
        (project_back(gate_grad_low, gate_w) + project_back(up_grad_low, up_w)).astype(
            jnp.bfloat16
        ),
        "tp",
    ).astype(jnp.float32)
    gate_w_grad = weight_grad(normed_two_low, gate_grad_low)
    up_w_grad = weight_grad(normed_two_low, up_grad_low)
    norm_back_two, gain_two_grad = rms_norm_back(normed_two_grad, gain_two_float, unit_two, inv_two)
    middle_grad = cotangent.astype(jnp.float32) + norm_back_two
    middle_low = middle_grad.astype(jnp.bfloat16)
    attended_grad_low = project_back(middle_low, out_w).astype(jnp.bfloat16)
    out_w_grad = weight_grad(attended_low, middle_low)
    out_grad = attended_grad_low.reshape(token_rows, kv_heads, groups, HD)
    delta_rows = jnp.transpose(jnp.sum(out_grad.astype(jnp.float32) * attended, axis=-1), (1, 2, 0))

    def backward_block(kv_block, source):
        visible = block_marks(source)
        return block_grads(queries, out_grad, kv_block, visible, log_total, delta_rows)

    query_start = jnp.zeros((token_rows, kv_heads, groups, HD), jnp.float32)

    def back_step(state_in, pieces):
        query_acc, kv_acc = state_in
        query_term, kv_term = backward_block(pieces[0], pieces[1])
        passed = shifted((kv_acc + kv_term).astype(jnp.bfloat16), "ctx", 1).astype(jnp.float32)
        return ((query_acc + query_term, passed), None)

    (query_grad, kv_grad), unused = lax.scan(
        back_step, (query_start, jnp.zeros(kv_local.shape, jnp.float32)), (kv_blocks, sources)
    )
    query_grad_low = (
        rotate_back(query_grad.reshape(token_rows, head_count, HD), cosine, sine)
        .reshape(token_rows, head_count * HD)
        .astype(jnp.bfloat16)
    )
    key_grad_low = (
        rotate_back(kv_grad[:, : kv_heads * HD].reshape(token_rows, kv_heads, HD), cosine, sine)
        .reshape(token_rows, kv_heads * HD)
        .astype(jnp.bfloat16)
    )
    value_grad_low = kv_grad[:, kv_heads * HD :].astype(jnp.bfloat16)
    normed_one_grad = lax.psum(
        (
            project_back(query_grad_low, query_w)
            + project_back(key_grad_low, key_w)
            + project_back(value_grad_low, value_w)
        ).astype(jnp.bfloat16),
        "tp",
    ).astype(jnp.float32)
    query_w_grad = weight_grad(normed_low, query_grad_low)
    key_w_grad = weight_grad(normed_low, key_grad_low)
    value_w_grad = weight_grad(normed_low, value_grad_low)
    norm_back_one, gain_one_grad = rms_norm_back(normed_one_grad, gain_one_float, unit_one, inv_one)
    input_grad = (middle_grad + norm_back_one).astype(jnp.bfloat16)
    summed = (
        lax.psum_scatter(
            gain_one_grad.astype(jnp.bfloat16), ("fsdp", "ctx"), scatter_dimension=0, tiled=True
        ).astype(jnp.float32),
        lax.psum_scatter(
            query_w_grad.astype(jnp.bfloat16), ("fsdp", "ctx"), scatter_dimension=0, tiled=True
        ).astype(jnp.float32),
        lax.psum_scatter(
            key_w_grad.astype(jnp.bfloat16), ("fsdp", "ctx"), scatter_dimension=0, tiled=True
        ).astype(jnp.float32),
        lax.psum_scatter(
            value_w_grad.astype(jnp.bfloat16), ("fsdp", "ctx"), scatter_dimension=0, tiled=True
        ).astype(jnp.float32),
        lax.psum_scatter(
            out_w_grad.astype(jnp.bfloat16), ("fsdp", "ctx"), scatter_dimension=1, tiled=True
        ).astype(jnp.float32),
        lax.psum_scatter(
            gain_two_grad.astype(jnp.bfloat16), ("fsdp", "ctx"), scatter_dimension=0, tiled=True
        ).astype(jnp.float32),
        lax.psum_scatter(
            gate_w_grad.astype(jnp.bfloat16), ("fsdp", "ctx"), scatter_dimension=0, tiled=True
        ).astype(jnp.float32),
        lax.psum_scatter(
            up_w_grad.astype(jnp.bfloat16), ("fsdp", "ctx"), scatter_dimension=0, tiled=True
        ).astype(jnp.float32),
        lax.psum_scatter(
            down_w_grad.astype(jnp.bfloat16), ("fsdp", "ctx"), scatter_dimension=1, tiled=True
        ).astype(jnp.float32),
    )
    return (output, input_grad) + tuple(summed)


def solution(mesh):
    in_specs = (
        P(("fsdp", "ctx"), None),
        P(("fsdp", "ctx")),
        P(("fsdp", "ctx"), "tp"),
        P(("fsdp", "ctx"), "tp"),
        P(("fsdp", "ctx"), "tp"),
        P("tp", ("fsdp", "ctx")),
        P(("fsdp", "ctx")),
        P(("fsdp", "ctx"), "tp"),
        P(("fsdp", "ctx"), "tp"),
        P("tp", ("fsdp", "ctx")),
        P(("fsdp", "ctx"), None),
        P(("fsdp", "ctx")),
        P(("fsdp", "ctx")),
    )
    out_specs = (
        P(("fsdp", "ctx"), None),
        P(("fsdp", "ctx"), None),
        P(("fsdp", "ctx")),
        P(("fsdp", "ctx"), "tp"),
        P(("fsdp", "ctx"), "tp"),
        P(("fsdp", "ctx"), "tp"),
        P("tp", ("fsdp", "ctx")),
        P(("fsdp", "ctx")),
        P(("fsdp", "ctx"), "tp"),
        P(("fsdp", "ctx"), "tp"),
        P("tp", ("fsdp", "ctx")),
    )
    return jax.shard_map(shards, mesh=mesh, in_specs=in_specs, out_specs=out_specs, check_vma=False)
```

profile of v0, /device:TPU:0, one launch (start us, length us, event | category | flops | bytes accessed | tf_op | source)
XLA Modules:
  0.0 1101.4 jit_solution(18198275863524223515)
XLA Ops:
  8.8 9.6 all-gather.1
  19.1 7.9 all-gather.2
  27.9 12.5 %all-gather = bf16[8,1,256]{2,1,0:T(2,128)(2,1)S(1)} all-gather(bf16[1,1,256]{2,1,0:T(2,128)(2,1)S(1)} %reshape.364), channel_id=1, replica_groups=mesh['fsdp'=2,'ctx'=4,'tp'=4] {'fsdp','ctx'}, dimensions={0}, use_global_device_ids=true | all-gather | bytes 4608 | tf_op jit(solution)/shard_map/all_gather | solution.py:173
  42.5 25.8 %all_gather.34 = bf16[2048,64]{0,1:T(8,128)(2,1)S(1)} all-gather(bf16[256,64]{0,1:T(8,128)(2,1)} %param.20), channel_id=1, replica_groups=mesh['fsdp'=2,'ctx'=4,'tp'=4] {'fsdp','ctx'}, dimensions={0}, use_global_device_ids=true | all-gather | bytes 294912 | tf_op jit(solution)/shard_map/all_gather | solution.py:175
  70.4 24.0 %all_gather.35 = bf16[2048,64]{0,1:T(8,128)(2,1)S(1)} all-gather(bf16[256,64]{0,1:T(8,128)(2,1)S(1)} %copy-done.36), channel_id=1, replica_groups=mesh['fsdp'=2,'ctx'=4,'tp'=4] {'fsdp','ctx'}, dimensions={0}, use_global_device_ids=true | all-gather | bytes 294912 | tf_op jit(solution)/shard_map/all_gather | solution.py:176
  95.5 3.5 fusion.126
  100.0 45.5 %while.34 = (s32[]{:T(128)}, f32[1,8,512]{2,1,0:T(8,128)S(1)}, f32[1,8,512]{2,1,0:T(8,128)S(1)}, f32[512,1,8,64]{0,3,2,1:T(8,128)}, bf16[512,128]{0,1:T(8,128)(2...) while((s32[]{:T(128)}, f32[1,8,512]{2,1,0:T(8,128)S(1)}, ...), condition=%wide.region_4.5_spmd.clone, body=%wide.region_1.4_spmd.clone.sunk | while | flops 565731328 | bytes 63848896 | solution.py:234
  107.1 6.8 fusion.193
  114.6 2.6 collective-permute-start
  123.6 7.0 fusion.193
  137.8 7.0 fusion.193
  145.5 2.5 fusion.49
  150.7 3.2 fusion.125
  153.9 4.4 convolution_convert_fusion.5
  160.1 14.7 %all-gather.3 = bf16[8,1,256]{2,1,0:T(2,128)(2,1)S(1)} all-gather(bf16[1,1,256]{2,1,0:T(2,128)(2,1)S(1)} %reshape.370), channel_id=1, replica_groups=mesh['fsdp'=2,'ctx'=4,'tp'=4] {'fsdp','ctx'}, dimensions={0}, use_global_device_ids=true | all-gather | bytes 4608 | tf_op jit(solution)/shard_map/all_gather | solution.py:180
  174.8 71.9 %all-reduce.8.cloned.1.call-done = bf16[512,2048]{1,0:T(8,128)(2,1)} async-done(((bf16[512,2048]{1,0:T(8,128)(2,1)}), bf16[512,2048]{1,0:T(8,128)(2,1)}) %all-reduce.8.cloned.1.call-update) | async-done | bytes 2097168 | tf_op jit(solution)/shard_map/psum | solution.py:244
  246.7 2.5 multiply_reduce_fusion
  249.2 2.4 multiply_convert_fusion
  251.6 39.3 %all-gather.14.cloned.1.call-done = bf16[2048,1408]{1,0:T(8,128)(2,1)} async-done(((bf16[256,1408]{1,0:T(8,128)(2,1)}), bf16[2048,1408]{1,0:T(8,128)(2,1)}) %all-gather.14.cloned.1.call-update) | async-done | bytes 5767184 | tf_op jit(solution)/shard_map/all_gather | solution.py:181
  290.9 8.2 fusion.127
  299.1 37.0 %all-gather.16.cloned.1.call-done = bf16[2048,1408]{1,0:T(8,128)(2,1)} async-done(((bf16[256,1408]{1,0:T(8,128)(2,1)}), bf16[2048,1408]{1,0:T(8,128)(2,1)}) %all-gather.16.cloned.1.call-update) | async-done | bytes 5767184 | tf_op jit(solution)/shard_map/all_gather | solution.py:182
  336.2 8.3 fusion.128
  344.4 38.0 %all-gather.18.cloned.1.call-done = bf16[1408,2048]{1,0:T(8,128)(2,1)} async-done(((bf16[1408,256]{1,0:T(8,128)(2,1)}), bf16[1408,2048]{1,0:T(8,128)(2,1)}) %all-gather.18.cloned.1.call-update) | async-done | bytes 5767184 | tf_op jit(solution)/shard_map/all_gather | solution.py:183
  382.4 10.4 multiply_convert_fusion.1
  392.8 6.6 fusion.129
  399.5 4.7 add_convert_fusion.1
  405.8 85.0 %all-reduce.10.cloned.1.call-done = bf16[512,2048]{1,0:T(8,128)(2,1)} async-done(((bf16[512,2048]{1,0:T(8,128)(2,1)}), bf16[512,2048]{1,0:T(8,128)(2,1)}) %all-reduce.10.cloned.1.call-update) | async-done | bytes 2097168 | tf_op jit(solution)/shard_map/psum | solution.py:264
  490.9 3.9 fusion.65
  495.0 4.7 convolution_convert_fusion.9
  501.0 84.5 %while.35 = (s32[]{:T(128)}, f32[512,1,8,64]{0,3,2,1:T(8,128)}, f32[512,128]{0,1:T(8,128)S(1)}, bf16[4,512,128]{1,2,0:T(8,128)(2,1)}, s32[512]{0:T(512)S(1)}, /*...) while((s32[]{:T(128)}, f32[512,1,8,64]{0,3,2,1:T(8,128)}, ...), condition=%wide.region_14.15_spmd.clone, body=%wide.region_13.14_spmd.clone.sunk | while | flops 1369276416 | bytes 45089044 | solution.py:292
  506.8 3.4 fusion.204
  510.3 4.4 fusion.202
  519.4 2.8 collective-permute-done.1
  528.2 3.4 fusion.204
  531.6 4.4 fusion.202
  538.0 3.1 fusion.203
  549.2 3.4 fusion.204
  552.6 4.4 fusion.202
  558.6 3.1 fusion.203
  561.7 2.6 collective-permute-done.1
  570.2 3.4 fusion.204
  573.7 4.4 fusion.202
  579.7 3.1 fusion.203
  582.8 2.6 collective-permute-done.1
  585.8 2.8 convolution_convert_fusion.8
  588.7 2.8 convolution_convert_fusion.7
  591.8 6.6 convolution_convert_fusion.3
  599.8 4.2 convolution_convert_fusion.4
  604.1 7.9 convolution_convert_fusion.6
  617.1 8.0 convolution_convert_fusion.2
  625.4 7.9 convolution_convert_fusion.1
  633.4 7.7 convolution_convert_fusion
  644.4 13.2 %reduce-scatter.12.cloned.1.call-done = bf16[256,64]{0,1:T(8,128)(2,1)} async-done(((bf16[2048,64]{0,1:T(8,128)(2,1)}), bf16[256,64]{0,1:T(8,128)(2,1)}) %reduce-scatter.12.cloned.1.call-update) | async-done | bytes 32784 | tf_op jit(solution)/shard_map/reduce_scatter | solution.py:329
  659.0 43.0 %reduce-scatter.14.cloned.1.call-done = bf16[512,256]{1,0:T(8,128)(2,1)} async-done(((bf16[512,2048]{1,0:T(8,128)(2,1)}), bf16[512,256]{1,0:T(8,128)(2,1)}) %reduce-scatter.14.cloned.1.call-update) | async-done | bytes 262160 | tf_op jit(solution)/shard_map/reduce_scatter | solution.py:332
  703.8 43.1 %reduce-scatter.8.cloned.1.call-done = bf16[256,512]{1,0:T(8,128)(2,1)} async-done(((bf16[2048,512]{1,0:T(8,128)(2,1)}), bf16[256,512]{1,0:T(8,128)(2,1)}) %reduce-scatter.8.cloned.1.call-update) | async-done | bytes 262160 | tf_op jit(solution)/shard_map/reduce_scatter | solution.py:323
  748.7 156.4 %all-reduce.12.cloned.1.call-done = (bf16[512,2048]{1,0:T(8,128)(2,1)}, bf16[512,2048]{1,0:T(8,128)(2,1)}) async-done(((bf16[512,2048]{1,0:T(8,128)(2,1)}, bf16[512,2048]{1,0:T(8,128)(2,1)}), (bf16[512,2048]{1,0:T(8,128)(2,1)}, bf16[512,2048]{1,0:T(8,128)(2,1)})) %all-reduce.12.cloned.1.call-update) | async-done | bytes 4194320 | tf_op jit(solution)/shard_map/psum | solution.py:253
  905.1 2.9 fusion.69
  908.0 14.7 %all-reduce.2 = (bf16[2048]{0:T(1024)(128)(2,1)S(1)}, bf16[2048]{0:T(1024)(128)(2,1)S(1)}) all-reduce(bf16[2048]{0:T(1024)(128)(2,1)S(1)} %get-tuple-element.338, bf16[2048]{0:T(1024)(128)(2,1)S(1)} %get-tuple-element.336), channel_id=2, replica_groups=mesh['fsdp'=2,'ctx'=4,'tp'=4] {'fsdp','ctx'}, use_global_device_ids=true, to_apply=%region_18.19.clone | all-reduce | flops 4096 | bytes 16384
  923.4 8.0 fusion.61
  931.4 35.6 %reduce-scatter.16.cloned.1.call-done = bf16[256,1408]{1,0:T(8,128)(2,1)} async-done(((bf16[2048,1408]{1,0:T(8,128)(2,1)}), bf16[256,1408]{1,0:T(8,128)(2,1)}) %reduce-scatter.16.cloned.1.call-update) | async-done | bytes 720912 | tf_op jit(solution)/shard_map/reduce_scatter | solution.py:338
  969.3 60.1 %reduce-scatter.18.cloned.1.call-done = bf16[256,1408]{1,0:T(8,128)(2,1)} async-done(((bf16[2048,1408]{1,0:T(8,128)(2,1)}), bf16[256,1408]{1,0:T(8,128)(2,1)}) %reduce-scatter.18.cloned.1.call-update) | async-done | bytes 720912 | tf_op jit(solution)/shard_map/reduce_scatter | solution.py:341
  1029.4 2.3 convert_element_type.227
  1031.7 60.4 %reduce-scatter.20.cloned.1.call-done = bf16[1408,256]{1,0:T(8,128)(2,1)} async-done(((bf16[1408,2048]{1,0:T(8,128)(2,1)}), bf16[1408,256]{1,0:T(8,128)(2,1)}) %reduce-scatter.20.cloned.1.call-update) | async-done | bytes 720912 | tf_op jit(solution)/shard_map/reduce_scatter | solution.py:344
  1092.1 2.3 convert_element_type.229
  (256 shorter events, 87.7 us)
Async XLA Ops:
  7.2 61.2 %copy-start.1 = (bf16[512,2048]{1,0:T(8,128)(2,1)S(1)}, bf16[512,2048]{1,0:T(8,128)(2,1)}, u32[]{:S(2)}) copy-start(bf16[512,2048]{1,0:T(8,128)(2,1)} %param.17) | copy-start | bytes 6291460
  7.2 88.3 %all-gather.10.cloned.1.call-start = ((), (), s32[]{:S(2)}) async-start(), calls=%async_computation.7 | async-start | bytes 2359296 | tf_op jit(solution)/shard_map/all_gather | solution.py:174
  7.9 146.0 %all-gather.12.cloned.1.call-start = ((), (), s32[]{:S(2)}) async-start(), calls=%async_computation.8 | async-start | bytes 2359296 | tf_op jit(solution)/shard_map/all_gather | solution.py:177
  8.7 238.0 %all-reduce.8.cloned.1.call-start = ((), (), s32[]{:S(2)}) async-start(), calls=%async_computation.9 | async-start | bytes 4194304 | tf_op jit(solution)/shard_map/psum | solution.py:244
  8.7 61.3 %copy-start.37 = (f32[32]{0:T(128)}, f32[32]{0:T(128)S(1)}, u32[]{:S(2)}) copy-start(f32[32]{0:T(128)S(1)} %multiply_power_fusion) | copy-start | bytes 388
  19.1 50.9 %copy-start.32 = (f32[512]{0:T(512)}, f32[512]{0:T(512)S(1)}, u32[]{:S(2)}) copy-start(f32[512]{0:T(512)S(1)} %convert_element_type.186) | copy-start | bytes 6148
  40.4 29.6 %copy-start.24 = (f32[8,1,256]{2,1,0:T(1,128)}, f32[8,1,256]{2,1,0:T(1,128)S(1)}, u32[]{:S(2)}) copy-start(f32[8,1,256]{2,1,0:T(1,128)S(1)} %convert_element_type.230) | copy-start | bytes 24580
  40.4 29.9 %copy-start.36 = (bf16[256,64]{0,1:T(8,128)(2,1)S(1)}, bf16[256,64]{0,1:T(8,128)(2,1)}, u32[]{:S(2)}) copy-start(bf16[256,64]{0,1:T(8,128)(2,1)} %param.21) | copy-start | bytes 98308
  42.5 52.6 %copy-start.30 = (f32[512]{0:T(512)}, f32[512]{0:T(512)S(1)}, u32[]{:S(2)}) copy-start(f32[512]{0:T(512)S(1)} %add_rsqrt_fusion.1) | copy-start | bytes 6148
  68.3 26.8 %copy-start.6 = (bf16[2048,64]{0,1:T(8,128)(2,1)}, bf16[2048,64]{0,1:T(8,128)(2,1)S(1)}, u32[]{:S(2)}) copy-start(bf16[2048,64]{0,1:T(8,128)(2,1)S(1)} %all_gather.34) | copy-start | bytes 786436
  68.3 26.8 %copy-start.20 = (s32[512]{0:T(512)S(1)}, s32[512]{0:T(512)}, u32[]{:S(2)}) copy-start(s32[512]{0:T(512)} %param.28) | copy-start | bytes 6148
  68.3 26.8 %copy-start.22 = (s32[512]{0:T(512)S(1)}, s32[512]{0:T(512)}, u32[]{:S(2)}) copy-start(s32[512]{0:T(512)} %param.29) | copy-start | bytes 6148
  68.9 25.5 %copy-start.2 = (bf16[512,2048]{1,0:T(8,128)(2,1)}, bf16[512,2048]{1,0:T(8,128)(2,1)S(1)}, u32[]{:S(2)}) copy-start(bf16[512,2048]{1,0:T(8,128)(2,1)S(1)} %fusion.67) | copy-start | bytes 6291460
  69.2 29.8 %copy-start.15 = (f32[512,32]{0,1:T(8,128)}, f32[512,32]{0,1:T(8,128)S(1)}, u32[]{:S(2)}) copy-start(f32[512,32]{0,1:T(8,128)S(1)} %get-tuple-element.416) | copy-start | bytes 196612
  69.2 29.8 %copy-start.17 = (f32[512,32]{0,1:T(8,128)}, f32[512,32]{0,1:T(8,128)S(1)}, u32[]{:S(2)}) copy-start(f32[512,32]{0,1:T(8,128)S(1)} %get-tuple-element.417) | copy-start | bytes 196612
  100.2 14.3 %collective-permute-start = (bf16[512,128]{0,1:T(8,128)(2,1)S(1)}, bf16[512,128]{0,1:T(8,128)(2,1)S(1)}, u32[]{:S(2)}, u32[]{:S(2)}) collective-permute-start(bf16[512,128]{0,1:T(8,128)(2,1)S(1)} %copy.50), channel_id=1, source_target_pairs={{0,4},{4,8},{8,12},{12,0},{1,5},{5,9},{9,13},{13,1},{2,6},{6,10},{... | collective-permute-start | bytes 393224 | tf_op jit(solution)/shard_map/while/body/eval_jaxpr/ppermute | solution.py:17
  103.8 3.3 copy-start
  114.6 16.7 %collective-permute-start = (bf16[512,128]{0,1:T(8,128)(2,1)S(1)}, bf16[512,128]{0,1:T(8,128)(2,1)S(1)}, u32[]{:S(2)}, u32[]{:S(2)}) collective-permute-start(bf16[512,128]{0,1:T(8,128)(2,1)S(1)} %copy.50), channel_id=1, source_target_pairs={{0,4},{4,8},{8,12},{12,0},{1,5},{5,9},{9,13},{13,1},{2,6},{6,10},{... | collective-permute-start | bytes 393224 | tf_op jit(solution)/shard_map/while/body/eval_jaxpr/ppermute | solution.py:17
  120.3 3.3 copy-start
  131.3 14.2 %collective-permute-start = (bf16[512,128]{0,1:T(8,128)(2,1)S(1)}, bf16[512,128]{0,1:T(8,128)(2,1)S(1)}, u32[]{:S(2)}, u32[]{:S(2)}) collective-permute-start(bf16[512,128]{0,1:T(8,128)(2,1)S(1)} %copy.50), channel_id=1, source_target_pairs={{0,4},{4,8},{8,12},{12,0},{1,5},{5,9},{9,13},{13,1},{2,6},{6,10},{... | collective-permute-start | bytes 393224 | tf_op jit(solution)/shard_map/while/body/eval_jaxpr/ppermute | solution.py:17
  134.5 3.3 copy-start
  145.5 2.5 copy-start.28
  145.5 2.5 copy-start.29
  148.0 2.7 copy-start.41
  153.9 6.2 copy-start.40
  158.3 132.6 %all-gather.14.cloned.1.call-start = ((), (), s32[]{:S(2)}) async-start(), calls=%async_computation.10 | async-start | bytes 6488064 | tf_op jit(solution)/shard_map/all_gather | solution.py:181
  158.9 177.3 %all-gather.16.cloned.1.call-start = ((), (), s32[]{:S(2)}) async-start(), calls=%async_computation.11 | async-start | bytes 6488064 | tf_op jit(solution)/shard_map/all_gather | solution.py:182
  159.5 222.9 %all-gather.18.cloned.1.call-start = ((), (), s32[]{:S(2)}) async-start(), calls=%async_computation.12 | async-start | bytes 6488064 | tf_op jit(solution)/shard_map/all_gather | solution.py:183
  160.1 330.8 %all-reduce.10.cloned.1.call-start = ((), (), s32[]{:S(2)}) async-start(), calls=%async_computation.13 | async-start | bytes 4194304 | tf_op jit(solution)/shard_map/psum | solution.py:264
  174.8 320.0 %copy-start.26 = (f32[8,1,256]{2,1,0:T(1,128)}, f32[8,1,256]{2,1,0:T(1,128)S(1)}, u32[]{:S(2)}) copy-start(f32[8,1,256]{2,1,0:T(1,128)S(1)} %convert_element_type.231) | copy-start | bytes 24580
  246.7 2.5 copy-start.3
  249.2 245.6 %copy-start.34 = (f32[512]{0:T(512)}, f32[512]{0:T(512)S(1)}, u32[]{:S(2)}) copy-start(f32[512]{0:T(512)S(1)} %add_rsqrt_fusion) | copy-start | bytes 6148
  392.8 6.6 copy-start.44
  392.8 6.6 copy-start.43
  392.8 6.6 copy-start.39
  399.5 5.5 copy-start.19
  404.2 238.8 %reduce-scatter.10.cloned.1.call-start = ((), (), s32[]{:S(2)}) async-start(), calls=%async_computation.15 | async-start | bytes 294912 | tf_op jit(solution)/shard_map/reduce_scatter | solution.py:326
  490.8 4.0 copy-start.4
  490.9 4.0 copy-start.5
  490.9 4.1 copy-start.10
  495.0 4.7 copy-start.12
  495.0 6.0 copy-start.21
  495.0 6.0 copy-start.23
  500.9 84.5 %copy-start.33 = (f32[512]{0:T(512)S(1)}, f32[512]{0:T(512)}, u32[]{:S(2)}) copy-start(f32[512]{0:T(512)} %copy-done.32) | copy-start | bytes 6148
  501.0 84.5 %copy-start.38 = (f32[32]{0:T(128)S(1)}, f32[32]{0:T(128)}, u32[]{:S(2)}) copy-start(f32[32]{0:T(128)} %copy-done.37) | copy-start | bytes 388
  516.1 6.2 collective-permute-start.1
  537.4 5.9 collective-permute-start.1
  558.4 5.9 collective-permute-start.1
  579.5 5.9 collective-permute-start.1
  585.4 6.3 copy-start.27
  585.4 6.3 copy-start.35
  588.6 69.0 %reduce-scatter.12.cloned.1.call-start = ((), (), s32[]{:S(2)}) async-start(), calls=%async_computation.16 | async-start | bytes 294912 | tf_op jit(solution)/shard_map/reduce_scatter | solution.py:329
  591.5 6.9 copy-start.16
  591.5 6.9 copy-start.18
  591.5 110.5 %reduce-scatter.14.cloned.1.call-start = ((), (), s32[]{:S(2)}) async-start(), calls=%async_computation.17 | async-start | bytes 2359296 | tf_op jit(solution)/shard_map/reduce_scatter | solution.py:332
  598.4 148.5 %reduce-scatter.8.cloned.1.call-start = ((), (), s32[]{:S(2)}) async-start(), calls=%async_computation.14 | async-start | bytes 2359296 | tf_op jit(solution)/shard_map/reduce_scatter | solution.py:323
  604.1 301.0 %all-reduce.12.cloned.1.call-start = ((), (), s32[]{:S(2)}) async-start(), calls=%async_computation.21 | async-start | bytes 8388608 | tf_op jit(solution)/shard_map/psum | solution.py:253
  604.1 7.9 copy-start.7
  612.0 1.6 copy-start.11
  617.0 350.0 %reduce-scatter.16.cloned.1.call-start = ((), (), s32[]{:S(2)}) async-start(), calls=%async_computation.18 | async-start | bytes 6488064 | tf_op jit(solution)/shard_map/reduce_scatter | solution.py:338
  625.1 404.3 %reduce-scatter.18.cloned.1.call-start = ((), (), s32[]{:S(2)}) async-start(), calls=%async_computation.19 | async-start | bytes 6488064 | tf_op jit(solution)/shard_map/reduce_scatter | solution.py:341
  633.3 458.8 %reduce-scatter.20.cloned.1.call-start = ((), (), s32[]{:S(2)}) async-start(), calls=%async_computation.20 | async-start | bytes 6488064 | tf_op jit(solution)/shard_map/reduce_scatter | solution.py:344
  641.1 264.0 %copy-start.25 = (f32[8,1,256]{2,1,0:T(1,128)S(1)}, f32[8,1,256]{2,1,0:T(1,128)}, u32[]{:S(2)}) copy-start(f32[8,1,256]{2,1,0:T(1,128)} %copy-done.24) | copy-start | bytes 24580
  641.1 264.0 %copy-start.31 = (f32[512]{0:T(512)S(1)}, f32[512]{0:T(512)}, u32[]{:S(2)}) copy-start(f32[512]{0:T(512)} %copy-done.30) | copy-start | bytes 6148
  (5 other events, 4.5 us)
Sparse Core Ops, SparseCore 0:
  9.9 30.6 all-gather.9
  42.5 29.3 all-gather.11
  158.4 88.2 all-reduce.7
  248.6 42.2 all-gather.13
  292.8 43.3 all-gather.15
  338.0 44.3 all-gather.17
  404.3 86.4 all-reduce.9
  588.7 31.8 reduce-scatter.9
  623.9 33.5 reduce-scatter.11
  660.7 41.2 reduce-scatter.13
  705.6 41.2 reduce-scatter.7
  749.7 155.3 all-reduce.11
  908.9 58.0 reduce-scatter.15
  970.3 59.0 reduce-scatter.17
  1033.0 58.9 reduce-scatter.19
where the time goes:
time: 1110 us; the launch traced here: 1100 us
  waiting for transfers between devices  697 us (63%)
  matrix products  188 us (17%)
  blocking collectives  109 us (10%)
  other arithmetic  53.5 us (5%)
  local copies, waits for them, and re-layouts  26.4 us (2%)
  between operations  15.7 us (1%)
    psum x1, waiting for transfers between devices, shards(): lax.psum(project(hidden_low, down_w).astype(jnp.bfloat16), 'tp')  156 us
    psum x1, waiting for transfers between devices, shards(): lax.psum((project_back(gate_grad_low, gate_w) + project_back(up_grad_low,...  85 us
    psum x1, waiting for transfers between devices, shards(): lax.psum(project(attended_low, out_w).astype(jnp.bfloat16), 'tp')  71.9 us
    reduce_scatter x1, waiting for transfers between devices, shards(): lax.psum_scatter(down_w_grad.astype(jnp.bfloat16), ('fsdp', 'ctx'), scatt...  60.4 us
    reduce_scatter x1, waiting for transfers between devices, shards(): lax.psum_scatter(up_w_grad.astype(jnp.bfloat16), ('fsdp', 'ctx'), scatter...  60.1 us
    reduce_scatter x1, waiting for transfers between devices, shards(): lax.psum_scatter(query_w_grad.astype(jnp.bfloat16), ('fsdp', 'ctx'), scat...  43.1 us
    reduce_scatter x1, waiting for transfers between devices, shards(): lax.psum_scatter(out_w_grad.astype(jnp.bfloat16), ('fsdp', 'ctx'), scatte...  43 us
    dot_general x7, matrix products, weight_grad(): lax.dot_general(left_side, right_side, (((0,), (0,)), ((), ())), preferre...  39.9 us
  transfers between devices with their start and end apart: 22, of which 16 were waited for; matrix products, arithmetic and copies ran while one was open for 15% of the time, Pallas kernels for 0%

commit v1 on v0

--- a/solution.py
+++ b/solution.py
@@ -250,9 +250,9 @@
     gate_lin = project(normed_two_low, gate_w)
     up_lin = project(normed_two_low, up_w)
     hidden_low = (jax.nn.silu(gate_lin) * up_lin).astype(jnp.bfloat16)
-    result = middle + lax.psum(project(hidden_low, down_w).astype(jnp.bfloat16), "tp").astype(
-        jnp.float32
-    )
+    result = middle + jnp.sum(
+        lax.all_gather(project(hidden_low, down_w).astype(jnp.bfloat16), "tp"), axis=0
+    ).astype(jnp.float32)
     output = result.astype(jnp.bfloat16)
     hidden_grad = project_back(cotangent, down_w)
     down_w_grad = weight_grad(hidden_low, cotangent)

time: 1110 us -> 1210 us (1.090)
  waiting for transfers between devices: 697 us -> 784 us
    all_gather x0 -> x1, waiting for transfers between devices: none -> 149 us  [shards(): lax.all_gather(project(hidden_low, down_w).astype(jnp.bfloat16), 'tp')]
    psum x1, waiting for transfers between devices: 156 us -> 87.4 us  [shards(): lax.psum((project_back(query_grad_low, query_w) + project_back(key_grad_l...]
    reduce_scatter x1, waiting for transfers between devices: 35.6 us -> 61.1 us  [shards(): lax.psum_scatter(gate_w_grad.astype(jnp.bfloat16), ('fsdp', 'ctx'), scatt...]
    reduce_scatter x1, waiting for transfers between devices: 43 us -> 25.5 us  [shards(): lax.psum_scatter(out_w_grad.astype(jnp.bfloat16), ('fsdp', 'ctx'), scatte...]
  transfers between devices with their start and end apart: 22 -> 23, of which waited for: 16 -> 17; matrix products, arithmetic and copies ran while one was open for 15% -> 13% of each run, Pallas kernels for 0% -> 0%
where the time goes in v1:
time: 1210 us; the launch traced here: 1200 us
  waiting for transfers between devices  784 us (65%)
  matrix products  192 us (16%)
  blocking collectives  110 us (9%)
  other arithmetic  60.7 us (5%)
  local copies, waits for them, and re-layouts  25 us (2%)
  between operations  15.6 us (1%)
    all_gather x1, waiting for transfers between devices, shards(): lax.all_gather(project(hidden_low, down_w).astype(jnp.bfloat16), 'tp')  149 us
    psum x1, waiting for transfers between devices, shards(): lax.psum((project_back(query_grad_low, query_w) + project_back(key_grad_l...  87.4 us
    psum x1, waiting for transfers between devices, shards(): lax.psum((project_back(gate_grad_low, gate_w) + project_back(up_grad_low,...  85 us
    psum x1, waiting for transfers between devices, shards(): lax.psum(project(attended_low, out_w).astype(jnp.bfloat16), 'tp')  71.8 us
    reduce_scatter x1, waiting for transfers between devices, shards(): lax.psum_scatter(gate_w_grad.astype(jnp.bfloat16), ('fsdp', 'ctx'), scatt...  61.1 us
    reduce_scatter x1, waiting for transfers between devices, shards(): lax.psum_scatter(down_w_grad.astype(jnp.bfloat16), ('fsdp', 'ctx'), scatt...  60.4 us
    reduce_scatter x1, waiting for transfers between devices, shards(): lax.psum_scatter(up_w_grad.astype(jnp.bfloat16), ('fsdp', 'ctx'), scatter...  60.1 us
    reduce_scatter x1, waiting for transfers between devices, shards(): lax.psum_scatter(query_w_grad.astype(jnp.bfloat16), ('fsdp', 'ctx'), scat...  42.6 us
  transfers between devices with their start and end apart: 23, of which 17 were waited for; matrix products, arithmetic and copies ran while one was open for 13% of the time, Pallas kernels for 0%

profile of v1, /device:TPU:0, one launch (start us, length us, event | category | flops | bytes accessed | tf_op | source)
XLA Modules:
  0.0 1199.1 jit_solution(11950769729936362534)
XLA Ops:
  8.8 9.6 all-gather.2
  19.1 7.9 all-gather.3
  27.9 12.5 %all-gather.1 = bf16[8,1,256]{2,1,0:T(2,128)(2,1)S(1)} all-gather(bf16[1,1,256]{2,1,0:T(2,128)(2,1)S(1)} %reshape.365), channel_id=1, replica_groups=mesh['fsdp'=2,'ctx'=4,'tp'=4] {'fsdp','ctx'}, dimensions={0}, use_global_device_ids=true | all-gather | bytes 4608 | tf_op jit(solution)/shard_map/all_gather | solution.py:173
  42.5 25.8 %all_gather.40 = bf16[2048,64]{0,1:T(8,128)(2,1)S(1)} all-gather(bf16[256,64]{0,1:T(8,128)(2,1)} %param.20), channel_id=1, replica_groups=mesh['fsdp'=2,'ctx'=4,'tp'=4] {'fsdp','ctx'}, dimensions={0}, use_global_device_ids=true | all-gather | bytes 294912 | tf_op jit(solution)/shard_map/all_gather | solution.py:175
  70.4 24.0 %all_gather.41 = bf16[2048,64]{0,1:T(8,128)(2,1)S(1)} all-gather(bf16[256,64]{0,1:T(8,128)(2,1)S(1)} %copy-done.36), channel_id=1, replica_groups=mesh['fsdp'=2,'ctx'=4,'tp'=4] {'fsdp','ctx'}, dimensions={0}, use_global_device_ids=true | all-gather | bytes 294912 | tf_op jit(solution)/shard_map/all_gather | solution.py:176
  95.5 3.5 fusion.126
  100.0 45.5 %while.34 = (s32[]{:T(128)}, f32[1,8,512]{2,1,0:T(8,128)S(1)}, f32[1,8,512]{2,1,0:T(8,128)S(1)}, f32[512,1,8,64]{0,3,2,1:T(8,128)}, bf16[512,128]{0,1:T(8,128)(2...) while((s32[]{:T(128)}, f32[1,8,512]{2,1,0:T(8,128)S(1)}, ...), condition=%wide.region_4.5_spmd.clone, body=%wide.region_1.4_spmd.clone.sunk | while | flops 565731328 | bytes 63848896 | solution.py:234
  107.2 6.8 fusion.193
  114.7 2.6 collective-permute-start
  123.7 7.0 fusion.193
  137.9 7.0 fusion.193
  150.7 3.2 fusion.125
  154.0 4.4 convolution_convert_fusion.5
  160.2 14.8 %all-gather.4 = bf16[8,1,256]{2,1,0:T(2,128)(2,1)S(1)} all-gather(bf16[1,1,256]{2,1,0:T(2,128)(2,1)S(1)} %reshape.371), channel_id=1, replica_groups=mesh['fsdp'=2,'ctx'=4,'tp'=4] {'fsdp','ctx'}, dimensions={0}, use_global_device_ids=true | all-gather | bytes 4608 | tf_op jit(solution)/shard_map/all_gather | solution.py:180
  175.0 71.8 %all-reduce.7.cloned.1.call-done = bf16[512,2048]{1,0:T(8,128)(2,1)} async-done(((bf16[512,2048]{1,0:T(8,128)(2,1)}), bf16[512,2048]{1,0:T(8,128)(2,1)}) %all-reduce.7.cloned.1.call-update) | async-done | bytes 2097168 | tf_op jit(solution)/shard_map/psum | solution.py:244
  246.8 2.5 multiply_reduce_fusion
  251.7 39.3 %all-gather.16.cloned.1.call-done = bf16[2048,1408]{1,0:T(8,128)(2,1)} async-done(((bf16[256,1408]{1,0:T(8,128)(2,1)}), bf16[2048,1408]{1,0:T(8,128)(2,1)}) %all-gather.16.cloned.1.call-update) | async-done | bytes 5767184 | tf_op jit(solution)/shard_map/all_gather | solution.py:181
  291.0 8.2 fusion.127
  299.2 37.0 %all-gather.18.cloned.1.call-done = bf16[2048,1408]{1,0:T(8,128)(2,1)} async-done(((bf16[256,1408]{1,0:T(8,128)(2,1)}), bf16[2048,1408]{1,0:T(8,128)(2,1)}) %all-gather.18.cloned.1.call-update) | async-done | bytes 5767184 | tf_op jit(solution)/shard_map/all_gather | solution.py:182
  336.2 8.3 fusion.128
  344.5 38.0 %all-gather.20.cloned.1.call-done = bf16[1408,2048]{1,0:T(8,128)(2,1)} async-done(((bf16[1408,256]{1,0:T(8,128)(2,1)}), bf16[1408,2048]{1,0:T(8,128)(2,1)}) %all-gather.20.cloned.1.call-update) | async-done | bytes 5767184 | tf_op jit(solution)/shard_map/all_gather | solution.py:183
  382.5 10.4 multiply_convert_fusion.1
  392.9 6.6 fusion.129
  399.5 4.7 add_convert_fusion.1
  405.9 85.0 %all-reduce.9.cloned.1.call-done = bf16[512,2048]{1,0:T(8,128)(2,1)} async-done(((bf16[512,2048]{1,0:T(8,128)(2,1)}), bf16[512,2048]{1,0:T(8,128)(2,1)}) %all-reduce.9.cloned.1.call-update) | async-done | bytes 2097168 | tf_op jit(solution)/shard_map/psum | solution.py:264
  490.9 3.9 fusion.65
  495.0 4.7 convolution_convert_fusion.9
  501.1 84.5 %while.35 = (s32[]{:T(128)}, f32[512,1,8,64]{0,3,2,1:T(8,128)}, f32[512,128]{0,1:T(8,128)S(1)}, bf16[4,512,128]{1,2,0:T(8,128)(2,1)}, s32[512]{0:T(512)S(1)}, /*...) while((s32[]{:T(128)}, f32[512,1,8,64]{0,3,2,1:T(8,128)}, ...), condition=%wide.region_14.15_spmd.clone, body=%wide.region_13.14_spmd.clone.sunk | while | flops 1369276416 | bytes 45089044 | solution.py:292
  507.0 3.4 fusion.204
  510.4 4.3 fusion.202
  519.6 2.8 collective-permute-done.1
  528.3 3.4 fusion.204
  531.7 4.3 fusion.202
  538.1 3.1 fusion.203
  549.4 3.4 fusion.204
  552.8 4.4 fusion.202
  558.8 3.1 fusion.203
  561.9 2.6 collective-permute-done.1
  570.4 3.4 fusion.204
  573.9 4.3 fusion.202
  579.9 3.1 fusion.203
  583.0 2.6 collective-permute-done.1
  585.7 2.8 convolution_convert_fusion.7
  588.8 2.8 convolution_convert_fusion.8
  593.3 2.8 fusion.110
  596.2 3.1 fusion.130
  601.4 6.5 convolution_convert_fusion.3
  608.0 4.2 convolution_convert_fusion.4
  612.3 8.0 convolution_convert_fusion.2
  620.8 7.9 convolution_convert_fusion.1
  628.8 7.7 convolution_convert_fusion
  636.6 7.9 convolution_convert_fusion.6
  647.2 13.4 %reduce-scatter.12.cloned.1.call-done = bf16[256,64]{0,1:T(8,128)(2,1)} async-done(((bf16[2048,64]{0,1:T(8,128)(2,1)}), bf16[256,64]{0,1:T(8,128)(2,1)}) %reduce-scatter.12.cloned.1.call-update) | async-done | bytes 32784 | tf_op jit(solution)/shard_map/reduce_scatter | solution.py:329
  662.0 87.4 %all-reduce.11.cloned.1.call-done = bf16[512,2048]{1,0:T(8,128)(2,1)} async-done(((bf16[512,2048]{1,0:T(8,128)(2,1)}), bf16[512,2048]{1,0:T(8,128)(2,1)}) %all-reduce.11.cloned.1.call-update) | async-done | bytes 2097168 | tf_op jit(solution)/shard_map/psum | solution.py:306
  749.3 2.9 fusion.69
  752.2 14.8 %all-reduce.2 = (bf16[2048]{0:T(1024)(128)(2,1)S(1)}, bf16[2048]{0:T(1024)(128)(2,1)S(1)}) all-reduce(bf16[2048]{0:T(1024)(128)(2,1)S(1)} %get-tuple-element.338, bf16[2048]{0:T(1024)(128)(2,1)S(1)} %get-tuple-element.336), channel_id=3, replica_groups=mesh['fsdp'=2,'ctx'=4,'tp'=4] {'fsdp','ctx'}, use_global_device_ids=true, to_apply=%region_18.19.clone | all-reduce | flops 4096 | bytes 16384
  767.7 25.5 %reduce-scatter.14.cloned.1.call-done = bf16[512,256]{1,0:T(8,128)(2,1)} async-done(((bf16[512,2048]{1,0:T(8,128)(2,1)}), bf16[512,256]{1,0:T(8,128)(2,1)}) %reduce-scatter.14.cloned.1.call-update) | async-done | bytes 262160 | tf_op jit(solution)/shard_map/reduce_scatter | solution.py:332
  795.0 42.6 %reduce-scatter.8.cloned.1.call-done = bf16[256,512]{1,0:T(8,128)(2,1)} async-done(((bf16[2048,512]{1,0:T(8,128)(2,1)}), bf16[256,512]{1,0:T(8,128)(2,1)}) %reduce-scatter.8.cloned.1.call-update) | async-done | bytes 262160 | tf_op jit(solution)/shard_map/reduce_scatter | solution.py:323
  839.4 61.1 %reduce-scatter.16.cloned.1.call-done = bf16[256,1408]{1,0:T(8,128)(2,1)} async-done(((bf16[2048,1408]{1,0:T(8,128)(2,1)}), bf16[256,1408]{1,0:T(8,128)(2,1)}) %reduce-scatter.16.cloned.1.call-update) | async-done | bytes 720912 | tf_op jit(solution)/shard_map/reduce_scatter | solution.py:338
  902.8 60.1 %reduce-scatter.18.cloned.1.call-done = bf16[256,1408]{1,0:T(8,128)(2,1)} async-done(((bf16[2048,1408]{1,0:T(8,128)(2,1)}), bf16[256,1408]{1,0:T(8,128)(2,1)}) %reduce-scatter.18.cloned.1.call-update) | async-done | bytes 720912 | tf_op jit(solution)/shard_map/reduce_scatter | solution.py:341
  965.1 60.4 %reduce-scatter.20.cloned.1.call-done = bf16[1408,256]{1,0:T(8,128)(2,1)} async-done(((bf16[1408,2048]{1,0:T(8,128)(2,1)}), bf16[1408,256]{1,0:T(8,128)(2,1)}) %reduce-scatter.20.cloned.1.call-update) | async-done | bytes 720912 | tf_op jit(solution)/shard_map/reduce_scatter | solution.py:344
  1027.9 149.3 %all-gather.22.cloned.1.call-done = bf16[2048,2048]{1,0:T(8,128)(2,1)} async-done(((bf16[512,2048]{1,0:T(8,128)(2,1)}), bf16[2048,2048]{1,0:T(8,128)(2,1)}) %all-gather.22.cloned.1.call-update) | async-done | bytes 8388624 | tf_op jit(solution)/shard_map/all_gather | solution.py:254
  1177.2 7.2 reduce_sum.103
  1184.4 8.0 fusion.61
  (260 shorter events, 94.0 us)
Async XLA Ops:
  7.2 61.2 %copy-start.1 = (bf16[512,2048]{1,0:T(8,128)(2,1)S(1)}, bf16[512,2048]{1,0:T(8,128)(2,1)}, u32[]{:S(2)}) copy-start(bf16[512,2048]{1,0:T(8,128)(2,1)} %param.17) | copy-start | bytes 6291460
  7.2 88.3 %all-gather.12.cloned.1.call-start = ((), (), s32[]{:S(2)}) async-start(), calls=%async_computation.7 | async-start | bytes 2359296 | tf_op jit(solution)/shard_map/all_gather | solution.py:174
  7.9 146.1 %all-gather.14.cloned.1.call-start = ((), (), s32[]{:S(2)}) async-start(), calls=%async_computation.8 | async-start | bytes 2359296 | tf_op jit(solution)/shard_map/all_gather | solution.py:177
  8.7 238.1 %all-reduce.7.cloned.1.call-start = ((), (), s32[]{:S(2)}) async-start(), calls=%async_computation.9 | async-start | bytes 4194304 | tf_op jit(solution)/shard_map/psum | solution.py:244
  8.7 61.3 %copy-start.37 = (f32[32]{0:T(128)}, f32[32]{0:T(128)S(1)}, u32[]{:S(2)}) copy-start(f32[32]{0:T(128)S(1)} %multiply_power_fusion) | copy-start | bytes 388
  19.1 50.9 %copy-start.32 = (f32[512]{0:T(512)}, f32[512]{0:T(512)S(1)}, u32[]{:S(2)}) copy-start(f32[512]{0:T(512)S(1)} %convert_element_type.188) | copy-start | bytes 6148
  40.4 29.6 %copy-start.24 = (f32[8,1,256]{2,1,0:T(1,128)}, f32[8,1,256]{2,1,0:T(1,128)S(1)}, u32[]{:S(2)}) copy-start(f32[8,1,256]{2,1,0:T(1,128)S(1)} %convert_element_type.232) | copy-start | bytes 24580
  40.4 29.9 %copy-start.36 = (bf16[256,64]{0,1:T(8,128)(2,1)S(1)}, bf16[256,64]{0,1:T(8,128)(2,1)}, u32[]{:S(2)}) copy-start(bf16[256,64]{0,1:T(8,128)(2,1)} %param.21) | copy-start | bytes 98308
  42.5 52.6 %copy-start.30 = (f32[512]{0:T(512)}, f32[512]{0:T(512)S(1)}, u32[]{:S(2)}) copy-start(f32[512]{0:T(512)S(1)} %add_rsqrt_fusion.1) | copy-start | bytes 6148
  68.3 26.8 %copy-start.9 = (bf16[2048,64]{0,1:T(8,128)(2,1)}, bf16[2048,64]{0,1:T(8,128)(2,1)S(1)}, u32[]{:S(2)}) copy-start(bf16[2048,64]{0,1:T(8,128)(2,1)S(1)} %all_gather.40) | copy-start | bytes 786436
  68.3 26.8 %copy-start.20 = (s32[512]{0:T(512)S(1)}, s32[512]{0:T(512)}, u32[]{:S(2)}) copy-start(s32[512]{0:T(512)} %param.28) | copy-start | bytes 6148
  68.3 26.8 %copy-start.22 = (s32[512]{0:T(512)S(1)}, s32[512]{0:T(512)}, u32[]{:S(2)}) copy-start(s32[512]{0:T(512)} %param.29) | copy-start | bytes 6148
  68.9 25.5 %copy-start.2 = (bf16[512,2048]{1,0:T(8,128)(2,1)}, bf16[512,2048]{1,0:T(8,128)(2,1)S(1)}, u32[]{:S(2)}) copy-start(bf16[512,2048]{1,0:T(8,128)(2,1)S(1)} %fusion.67) | copy-start | bytes 6291460
  69.2 29.8 %copy-start.15 = (f32[512,32]{0,1:T(8,128)}, f32[512,32]{0,1:T(8,128)S(1)}, u32[]{:S(2)}) copy-start(f32[512,32]{0,1:T(8,128)S(1)} %get-tuple-element.414) | copy-start | bytes 196612
  69.2 29.8 %copy-start.17 = (f32[512,32]{0,1:T(8,128)}, f32[512,32]{0,1:T(8,128)S(1)}, u32[]{:S(2)}) copy-start(f32[512,32]{0,1:T(8,128)S(1)} %get-tuple-element.415) | copy-start | bytes 196612
  100.3 14.3 %collective-permute-start = (bf16[512,128]{0,1:T(8,128)(2,1)S(1)}, bf16[512,128]{0,1:T(8,128)(2,1)S(1)}, u32[]{:S(2)}, u32[]{:S(2)}) collective-permute-start(bf16[512,128]{0,1:T(8,128)(2,1)S(1)} %copy.50), channel_id=1, source_target_pairs={{0,4},{4,8},{8,12},{12,0},{1,5},{5,9},{9,13},{13,1},{2,6},{6,10},{... | collective-permute-start | bytes 393224 | tf_op jit(solution)/shard_map/while/body/eval_jaxpr/ppermute | solution.py:17
  103.9 3.3 copy-start
  114.7 16.7 %collective-permute-start = (bf16[512,128]{0,1:T(8,128)(2,1)S(1)}, bf16[512,128]{0,1:T(8,128)(2,1)S(1)}, u32[]{:S(2)}, u32[]{:S(2)}) collective-permute-start(bf16[512,128]{0,1:T(8,128)(2,1)S(1)} %copy.50), channel_id=1, source_target_pairs={{0,4},{4,8},{8,12},{12,0},{1,5},{5,9},{9,13},{13,1},{2,6},{6,10},{... | collective-permute-start | bytes 393224 | tf_op jit(solution)/shard_map/while/body/eval_jaxpr/ppermute | solution.py:17
  120.4 3.3 copy-start
  131.3 14.2 %collective-permute-start = (bf16[512,128]{0,1:T(8,128)(2,1)S(1)}, bf16[512,128]{0,1:T(8,128)(2,1)S(1)}, u32[]{:S(2)}, u32[]{:S(2)}) collective-permute-start(bf16[512,128]{0,1:T(8,128)(2,1)S(1)} %copy.50), channel_id=1, source_target_pairs={{0,4},{4,8},{8,12},{12,0},{1,5},{5,9},{9,13},{13,1},{2,6},{6,10},{... | collective-permute-start | bytes 393224 | tf_op jit(solution)/shard_map/while/body/eval_jaxpr/ppermute | solution.py:17
  134.6 3.3 copy-start
  145.5 2.5 copy-start.29
  148.0 2.7 copy-start.41
  154.0 6.2 copy-start.40
  158.4 132.6 %all-gather.16.cloned.1.call-start = ((), (), s32[]{:S(2)}) async-start(), calls=%async_computation.10 | async-start | bytes 6488064 | tf_op jit(solution)/shard_map/all_gather | solution.py:181
  159.0 177.2 %all-gather.18.cloned.1.call-start = ((), (), s32[]{:S(2)}) async-start(), calls=%async_computation.11 | async-start | bytes 6488064 | tf_op jit(solution)/shard_map/all_gather | solution.py:182
  159.5 222.9 %all-gather.20.cloned.1.call-start = ((), (), s32[]{:S(2)}) async-start(), calls=%async_computation.12 | async-start | bytes 6488064 | tf_op jit(solution)/shard_map/all_gather | solution.py:183
  160.1 330.8 %all-reduce.9.cloned.1.call-start = ((), (), s32[]{:S(2)}) async-start(), calls=%async_computation.13 | async-start | bytes 4194304 | tf_op jit(solution)/shard_map/psum | solution.py:264
  175.0 319.9 %copy-start.26 = (f32[8,1,256]{2,1,0:T(1,128)}, f32[8,1,256]{2,1,0:T(1,128)S(1)}, u32[]{:S(2)}) copy-start(f32[8,1,256]{2,1,0:T(1,128)S(1)} %convert_element_type.233) | copy-start | bytes 24580
  246.8 2.5 copy-start.3
  249.3 245.6 %copy-start.34 = (f32[512]{0:T(512)}, f32[512]{0:T(512)S(1)}, u32[]{:S(2)}) copy-start(f32[512]{0:T(512)S(1)} %add_rsqrt_fusion) | copy-start | bytes 6148
  392.9 6.6 copy-start.44
  392.9 6.6 copy-start.43
  392.9 6.6 copy-start.39
  399.5 5.6 copy-start.19
  404.2 241.5 %reduce-scatter.10.cloned.1.call-start = ((), (), s32[]{:S(2)}) async-start(), calls=%async_computation.16 | async-start | bytes 294912 | tf_op jit(solution)/shard_map/reduce_scatter | solution.py:326
  490.9 4.0 copy-start.4
  490.9 4.0 copy-start.6
  490.9 4.1 copy-start.11
  495.0 4.7 copy-start.12
  495.0 6.0 copy-start.21
  495.0 6.0 copy-start.23
  501.0 87.5 %copy-start.33 = (f32[512]{0:T(512)S(1)}, f32[512]{0:T(512)}, u32[]{:S(2)}) copy-start(f32[512]{0:T(512)} %copy-done.32) | copy-start | bytes 6148
  501.1 87.4 %copy-start.38 = (f32[32]{0:T(128)S(1)}, f32[32]{0:T(128)}, u32[]{:S(2)}) copy-start(f32[32]{0:T(128)} %copy-done.37) | copy-start | bytes 388
  516.2 6.2 collective-permute-start.1
  537.5 5.9 collective-permute-start.1
  558.6 5.9 collective-permute-start.1
  579.7 5.9 collective-permute-start.1
  585.6 6.3 copy-start.16
  585.6 6.3 copy-start.18
  585.6 7.7 copy-start.10
  591.6 68.9 %reduce-scatter.12.cloned.1.call-start = ((), (), s32[]{:S(2)}) async-start(), calls=%async_computation.17 | async-start | bytes 294912 | tf_op jit(solution)/shard_map/reduce_scatter | solution.py:329
  596.1 153.2 %all-reduce.11.cloned.1.call-start = ((), (), s32[]{:S(2)}) async-start(), calls=%async_computation.14 | async-start | bytes 4194304 | tf_op jit(solution)/shard_map/psum | solution.py:306
  596.2 3.1 copy-start.5
  596.2 3.1 copy-start.8
  601.4 191.8 %reduce-scatter.14.cloned.1.call-start = ((), (), s32[]{:S(2)}) async-start(), calls=%async_computation.18 | async-start | bytes 2359296 | tf_op jit(solution)/shard_map/reduce_scatter | solution.py:332
  608.0 229.6 %reduce-scatter.8.cloned.1.call-start = ((), (), s32[]{:S(2)}) async-start(), calls=%async_computation.15 | async-start | bytes 2359296 | tf_op jit(solution)/shard_map/reduce_scatter | solution.py:323
  612.3 288.2 %reduce-scatter.16.cloned.1.call-start = ((), (), s32[]{:S(2)}) async-start(), calls=%async_computation.19 | async-start | bytes 6488064 | tf_op jit(solution)/shard_map/reduce_scatter | solution.py:338
  620.4 342.5 %reduce-scatter.18.cloned.1.call-start = ((), (), s32[]{:S(2)}) async-start(), calls=%async_computation.20 | async-start | bytes 6488064 | tf_op jit(solution)/shard_map/reduce_scatter | solution.py:341
  628.7 396.8 %reduce-scatter.20.cloned.1.call-start = ((), (), s32[]{:S(2)}) async-start(), calls=%async_computation.21 | async-start | bytes 6488064 | tf_op jit(solution)/shard_map/reduce_scatter | solution.py:344
  636.5 8.0 copy-start.42
  636.6 112.8 %copy-start.25 = (f32[8,1,256]{2,1,0:T(1,128)S(1)}, f32[8,1,256]{2,1,0:T(1,128)}, u32[]{:S(2)}) copy-start(f32[8,1,256]{2,1,0:T(1,128)} %copy-done.24) | copy-start | bytes 24580
  636.6 112.8 %copy-start.31 = (f32[512]{0:T(512)S(1)}, f32[512]{0:T(512)}, u32[]{:S(2)}) copy-start(f32[512]{0:T(512)} %copy-done.30) | copy-start | bytes 6148
  636.6 540.7 %all-gather.22.cloned.1.call-start = ((), (), s32[]{:S(2)}) async-start(), calls=%async_computation.22 | async-start | bytes 10485760 | tf_op jit(solution)/shard_map/all_gather | solution.py:254
  (6 other events, 9.3 us)
Sparse Core Ops, SparseCore 0:
  9.9 30.6 all-gather.11
  42.5 29.3 all-gather.13
  158.5 88.2 all-reduce.6
  248.7 42.2 all-gather.15
  292.8 43.3 all-gather.17
  338.1 44.3 all-gather.19
  404.4 86.5 all-reduce.8
  591.7 31.8 reduce-scatter.9
  626.9 33.5 reduce-scatter.11
  662.8 86.5 all-reduce.10
  753.0 40.1 reduce-scatter.13
  796.3 41.1 reduce-scatter.7
  841.4 59.0 reduce-scatter.15
  903.8 59.0 reduce-scatter.17
  966.5 58.9 reduce-scatter.19
  1027.6 149.6 all-gather.21
